TPU v7x, 512 devices: a whole 4x4x16 slice. The times are simulated.
512 devices in a mesh: ad: 64 (over z, x), tp: 8 (over y, core).
Axes of the slice: x: 4, y: 4, z: 16, core: 2. Of those that a mesh axis runs over, the one named last changes fastest.
Arguments:
- tokens: bfloat16 [4, 3072, 8192], P(None, 'ad', 'tp'), may hold values from -6 to 6
- row_adapter_index: int32 [4, 3072], P(None, 'ad'), may hold values from 0 to 255, as said below
- key_base_weight: bfloat16 [8192, 1024], P('tp'), may hold values from -0.0625 to 0.0625
- adapter_down_weight: bfloat16 [256, 8192, 64], P('ad', 'tp'), may hold values from -0.0625 to 0.0625
- adapter_up_weight: bfloat16 [256, 64, 1024], P('ad', None, 'tp'), may hold values from -0.75 to 0.75
Outputs:
- token_keys_output: bfloat16 [4, 3072, 1024], P(None, 'ad', 'tp')
Inputs may be any that keep to these rules, and one draw needn't show every extreme that they name: `row_adapter_index`: group g holds adapters g * 4 to (g + 1) * 4 - 1. In each step the 48 rows of one index of ad name one group in exactly 2 rows and every other group in at most 1 row; that busiest group is the same for every index of ad in a step, so it receives 2 rows from each.
All inputs are finite; a program needn't handle non-finite values.
Results may differ from a plain program's by a relative error of at most 0.005.
Values may be sent and summed in bfloat16 or wider, within the bound.
A program may use at most 64 MiB of HBM per device.

v0:
```python
import jax
import jax.numpy as jnp
from jax import lax
from jax.sharding import PartitionSpec as P

TAG_WIDTH = 128


def body(tokens, row_adapter_index, key_base_weight, adapter_down_weight, adapter_up_weight):
    step_count, row_dev, width_per_shard = tokens.shape
    groups = lax.axis_size("ad")
    me = lax.axis_index("ad")
    adapter_number = adapter_down_weight.shape[0]
    rank = adapter_down_weight.shape[2]
    row_total = step_count * row_dev
    regular_total = groups * step_count
    wide = width_per_shard + TAG_WIDTH
    gathered_rows = tokens.reshape(row_total, width_per_shard)
    index_list = row_adapter_index.reshape(step_count, row_dev)
    owner_group = index_list // adapter_number
    local_index = index_list % adapter_number
    group_hits = (
        owner_group[:, :, None] == jnp.arange(groups, dtype=jnp.int32)[None, None, :]
    ).astype(jnp.int32)
    slot_rank = jnp.sum((jnp.cumsum(group_hits, axis=1) - group_hits) * group_hits, axis=2)
    step_ids = jnp.arange(step_count, dtype=jnp.int32)[:, None]
    first = slot_rank == 0
    regular_slot = jnp.where(first, owner_group * step_count + step_ids, -1).reshape(row_total)
    overflow_slot = jnp.where(slot_rank == 1, step_ids, -1).reshape(row_total)
    dispatch = (
        regular_slot[None, :] == jnp.arange(regular_total, dtype=jnp.int32)[:, None]
    ).astype(jnp.bfloat16)
    dispatch_over = (
        overflow_slot[None, :] == jnp.arange(step_count, dtype=jnp.int32)[:, None]
    ).astype(jnp.bfloat16)
    tag_values = jnp.where(first, local_index + 1, index_list + 1).astype(jnp.bfloat16)
    tag_block = jnp.broadcast_to(tag_values.reshape(row_total, 1), (row_total, TAG_WIDTH))
    rows_tagged = jnp.concatenate([gathered_rows, tag_block], axis=1)
    send_rows = jnp.dot(dispatch, rows_tagged, preferred_element_type=jnp.float32).astype(
        jnp.bfloat16
    )
    send_rows = send_rows.reshape(groups, step_count, wide)
    send_over = jnp.dot(dispatch_over, rows_tagged, preferred_element_type=jnp.float32).astype(
        jnp.bfloat16
    )
    incoming_over = lax.all_gather(send_over, "ad", tiled=True)
    incoming = lax.all_to_all(send_rows, "ad", split_axis=0, concat_axis=0, tiled=True)
    partial_base = jnp.dot(gathered_rows, key_base_weight, preferred_element_type=jnp.float32)
    partial_base, incoming_over = lax.optimization_barrier((partial_base, incoming_over))
    base_keys_output = lax.psum_scatter(partial_base, "tp", scatter_dimension=1, tiled=True)
    key_feature_width = base_keys_output.shape[1]
    incoming = jnp.concatenate([incoming.reshape(regular_total, wide), incoming_over], axis=0)
    slot_total = incoming.shape[0]
    incoming_rows = incoming[:, :width_per_shard]
    regular_labels = incoming[:regular_total, width_per_shard].astype(jnp.float32)
    over_labels = incoming[regular_total:, width_per_shard].astype(jnp.float32) - (
        me * adapter_number
    ).astype(jnp.float32)
    incoming_labels = jnp.concatenate([regular_labels, over_labels])
    down_all = jnp.einsum(
        "nd,adr->nar", incoming_rows, adapter_down_weight, preferred_element_type=jnp.float32
    )
    labels = (jnp.arange(adapter_number, dtype=jnp.int32) + 1).astype(jnp.float32)
    selector = (incoming_labels[:, None] == labels[None, :]).astype(jnp.float32)
    down_part = jnp.sum(down_all * selector[:, :, None], axis=1)
    down_sum = lax.psum(down_part, "tp")
    down_low = down_sum.astype(jnp.bfloat16)
    spread_rows = (selector.astype(jnp.bfloat16)[:, :, None] * down_low[:, None, :]).reshape(
        slot_total, adapter_number * rank
    )
    up_flat = adapter_up_weight.reshape(adapter_number * rank, key_feature_width)
    adapter_update = jnp.dot(spread_rows, up_flat, preferred_element_type=jnp.float32).astype(
        jnp.bfloat16
    )
    update_regular = adapter_update[:regular_total].reshape(groups, step_count, key_feature_width)
    update_over = adapter_update[regular_total:].reshape(groups, step_count, key_feature_width)
    send_back = jnp.concatenate([update_regular, update_over], axis=1)
    rows_sent_back = lax.all_to_all(send_back, "ad", split_axis=0, concat_axis=0, tiled=True)
    back_regular = rows_sent_back[:, :step_count].reshape(regular_total, key_feature_width)
    back_over = jnp.sum(rows_sent_back[:, step_count:].astype(jnp.float32), axis=0)
    routed = jnp.dot(dispatch.T, back_regular, preferred_element_type=jnp.float32) + jnp.dot(
        dispatch_over.T.astype(jnp.float32), back_over, preferred_element_type=jnp.float32
    )
    out = (base_keys_output + routed).astype(jnp.bfloat16)
    return out.reshape(step_count, row_dev, key_feature_width)


def solution(mesh):
    placed = (
        P(None, "ad", "tp"),
        P(None, "ad"),
        P("tp", None),
        P("ad", "tp", None),
        P("ad", None, "tp"),
    )
    return jax.shard_map(
        body, mesh=mesh, in_specs=placed, out_specs=P(None, "ad", "tp"), check_vma=False
    )
```

profile of v0, /device:TPU:2, one launch (start us, length us, event | category | flops | bytes accessed | tf_op | source)
XLA Modules:
  0.0 221.5 jit_solution(2728375814923560662)
XLA Ops:
  6.5 0.8 add_select_fusion.1
  7.4 0.1 fusion.11
  7.5 0.1 reduce_window_sum.11
  7.6 0.2 select_reduce_fusion
  7.8 0.7 add_select_fusion.2
  8.5 0.7 fusion.15
  9.2 0.1 broadcast_in_dim.19
  9.3 0.1 eq.83
  9.4 0.1 broadcast_in_dim.20
  9.5 1.3 convolution_convert_fusion
  10.8 1.0 reshape.110
  11.8 18.6 %all-to-all-start = ((bf16[64,4,1152]{2,1,0:T(4,128)(2,1)}), bf16[64,4,1152]{2,1,0:T(4,128)(2,1)S(1)}, u32[]{:S(2)}, u32[]{:S(2)}) async-start(bf16[64,4,1152]{2,1,0:T(4,128)(2,1)} %reshape.110), calls=%async_computation.1 | async-start | bytes 1179648 | tf_op jit(solution)/shard_map/all_to_all | solution.py:47
  30.4 0.0 reduce-scatter.2.cloned.1.call-start
  30.5 0.1 select_n.32
  30.6 0.2 fusion
  30.7 120.6 %all-gather = bf16[64,4,1152]{2,1,0:T(4,128)(2,1)S(1)} all-gather(bf16[1,4,1152]{2,1,0:T(4,128)(2,1)S(1)} %fusion), channel_id=1, replica_groups=mesh['ad'=64,'tp'=8] {'ad'}, dimensions={0}, use_global_device_ids=true | all-gather | bytes 599040 | tf_op jit(solution)/shard_map/all_gather | solution.py:46
  151.3 1.0 reshape.118
  152.3 2.5 %fusion.25 = f32[192,1024]{1,0:T(8,128)} fusion(bf16[192,1024]{1,0:T(8,128)(2,1)} %bitcast.23, bf16[1024,1024]{1,0:T(8,128)(2,1)S(1)} %copy-done), kind=kOutput, calls=%fused_computation.52 | convolution fusion | flops 402653184 | bytes 3276800 | tf_op jit(solution)/shard_map/dot_general | solution.py:48
  154.8 0.0 reduce-scatter.2.cloned.1.call-update
  154.9 0.1 subtract_reduce_fusion
  155.0 1.0 reshape.111
  156.0 1.0 convert_reduce_fusion
  156.9 1.7 fusion.4
  158.7 0.1 fusion.23
  158.7 0.1 multiply_reduce_fusion
  158.8 24.9 %all-reduce.1 = bf16[512,64]{0,1:T(8,128)(2,1)S(1)} all-reduce(f32[512,64]{0,1:T(8,128)S(1)} %multiply_reduce_fusion), channel_id=1, replica_groups=mesh['ad'=64,'tp'=8] {'tp'}, use_global_device_ids=true, to_apply=%region_4.5 | all-reduce | flops 32768 | bytes 196608 | tf_op jit(solution)/shard_map/psum | solution.py:66
  183.7 0.3 fusion.1
  184.0 0.1 pad_maximum_fusion.5
  184.0 28.5 %all_to_all.10 = bf16[64,8,128]{2,1,0:T(8,128)(2,1)S(1)} all-to-all(bf16[64,8,128]{2,1,0:T(8,128)(2,1)S(1)} %pad_maximum_fusion.5), channel_id=1, replica_groups=mesh['ad'=64,'tp'=8] {'ad'}, dimensions={0} | all-to-all | bytes 262144 | tf_op jit(solution)/shard_map/all_to_all | solution.py:78
  212.6 0.1 convert_reduce_fusion.1
  212.6 0.2 fusion.12
  212.9 1.8 fusion.3
  (14 shorter events, 0.1 us)
Async XLA Ops:
  6.5 145.8 %copy-start = (bf16[1024,1024]{1,0:T(8,128)(2,1)S(1)}, bf16[1024,1024]{1,0:T(8,128)(2,1)}, u32[]{:S(2)}) copy-start(bf16[1024,1024]{1,0:T(8,128)(2,1)} %param.7) | copy-start | bytes 6291460
  6.5 24.0 %copy-start.2 = (bf16[4,48,1024]{2,1,0:T(8,128)(2,1)S(1)}, bf16[4,48,1024]{2,1,0:T(8,128)(2,1)}, u32[]{:S(2)}) copy-start(bf16[4,48,1024]{2,1,0:T(8,128)(2,1)} %param.5) | copy-start | bytes 1179652
  11.8 143.2 %all-to-all-start = ((bf16[64,4,1152]{2,1,0:T(4,128)(2,1)}), bf16[64,4,1152]{2,1,0:T(4,128)(2,1)S(1)}, u32[]{:S(2)}, u32[]{:S(2)}) async-start(bf16[64,4,1152]{2,1,0:T(4,128)(2,1)} %reshape.110), calls=%async_computation.1 | async-start | bytes 1179648 | tf_op jit(solution)/shard_map/all_to_all | solution.py:47
  30.4 182.5 %reduce-scatter.2.cloned.1.call-start = ((), (), s32[]{:S(2)}) async-start(), calls=%async_computation.3 | async-start | bytes 884736 | tf_op jit(solution)/shard_map/reduce_scatter | solution.py:50
  152.3 2.6 %copy-start.1 = (bf16[256,1152]{1,0:T(8,128)(2,1)S(1)}, bf16[256,1152]{1,0:T(8,128)(2,1)}, u32[]{:S(2)}) copy-start(bf16[256,1152]{1,0:T(8,128)(2,1)} %reshape.118) | copy-start | bytes 1769476
  156.0 27.7 %copy-start.3 = (bf16[4,64,128]{2,1,0:T(8,128)(2,1)S(1)}, bf16[4,64,128]{2,1,0:T(8,128)(2,1)}, u32[]{:S(2)}) copy-start(bf16[4,64,128]{2,1,0:T(8,128)(2,1)} %param.9) | copy-start | bytes 196612
Sparse Core Ops, SparseCore 0:
  155.0 38.6 reduce-scatter.1
where the time goes:
time: 222 us; the launch traced here: 221 us
  blocking collectives  174 us (78%)
  starting transfers between devices  18.7 us (8%)
  between operations  13.5 us (6%)
  matrix products  7.98 us (4%)
  other arithmetic  4.05 us (2%)
  local copies, waits for them, and re-layouts  3.28 us (1%)
    all_gather x1, blocking collectives, body(): incoming_over = lax.all_gather(send_over, 'ad', tiled=True)  121 us
    all_to_all x1, blocking collectives, body(): lax.all_to_all(send_back, 'ad', split_axis=0, concat_axis=0, tiled=True)  28.5 us
    psum x1, blocking collectives, body(): down_sum = lax.psum(down_part, 'tp')  24.9 us
    all_to_all x1, starting transfers between devices, body(): lax.all_to_all(send_rows, 'ad', split_axis=0, concat_axis=0, tiled=True)  18.6 us
  transfers between devices with their start and end apart: 2, of which 0 were waited for; matrix products, arithmetic and copies ran while one was open for 4% of the time, Pallas kernels for 0%

commit v1 on v0

--- a/solution.py
+++ b/solution.py
@@ -63,7 +63,8 @@
     labels = (jnp.arange(adapter_number, dtype=jnp.int32) + 1).astype(jnp.float32)
     selector = (incoming_labels[:, None] == labels[None, :]).astype(jnp.float32)
     down_part = jnp.sum(down_all * selector[:, :, None], axis=1)
-    down_sum = lax.psum(down_part, "tp")
+    terms = lax.all_gather(down_part, "tp")
+    down_sum = jnp.sum(terms, axis=0)
     down_low = down_sum.astype(jnp.bfloat16)
     spread_rows = (selector.astype(jnp.bfloat16)[:, :, None] * down_low[:, None, :]).reshape(
         slot_total, adapter_number * rank

time: 222 us -> 241 us (1.086)
  waiting for transfers between devices: 0.03 us -> 37.6 us
  blocking collectives: 174 us -> 153 us
    all_gather x0 -> x1, waiting for transfers between devices: none -> 29.5 us  [body(): terms = lax.all_gather(down_part, 'tp')]
    psum x1 -> x0, blocking collectives: 24.9 us -> none  [body(): down_sum = lax.psum(down_part, 'tp')]
    reduce_scatter x1, waiting for transfers between devices: 0.02 us -> 7.39 us  [body(): lax.psum_scatter(partial_base, 'tp', scatter_dimension=1, tiled=True)]
    all_to_all x1, blocking collectives: 28.5 us -> 32.5 us  [body(): lax.all_to_all(send_back, 'ad', split_axis=0, concat_axis=0, tiled=True)]
  transfers between devices with their start and end apart: 2 -> 3, of which waited for: 0 -> 2; matrix products, arithmetic and copies ran while one was open for 4% -> 3% of each run, Pallas kernels for 0% -> 0%
where the time goes in v1:
time: 241 us
  blocking collectives  153 us (63%)
  waiting for transfers between devices  37.6 us (16%)
  starting transfers between devices  18.7 us (8%)
  between operations  13.5 us (6%)
  matrix products  7.96 us (3%)
  local copies, waits for them, and re-layouts  5.11 us (2%)
  other arithmetic  4.93 us (2%)
    all_gather x1, blocking collectives, body(): incoming_over = lax.all_gather(send_over, 'ad', tiled=True)  121 us
    all_to_all x1, blocking collectives, body(): lax.all_to_all(send_back, 'ad', split_axis=0, concat_axis=0, tiled=True)  32.5 us
    all_gather x1, waiting for transfers between devices, body(): terms = lax.all_gather(down_part, 'tp')  29.5 us
    all_to_all x1, starting transfers between devices, body(): lax.all_to_all(send_rows, 'ad', split_axis=0, concat_axis=0, tiled=True)  18.6 us
    reduce_scatter x1, waiting for transfers between devices, body(): lax.psum_scatter(partial_base, 'tp', scatter_dimension=1, tiled=True)  7.39 us
  transfers between devices with their start and end apart: 3, of which 2 were waited for; matrix products, arithmetic and copies ran while one was open for 3% of the time, Pallas kernels for 0%

profile of v1, /device:TPU:2, one launch (start us, length us, event | category | flops | bytes accessed | tf_op | source)
XLA Modules:
  0.0 241.0 jit_solution(18104021679790323151)
XLA Ops:
  6.5 0.8 add_select_fusion.1
  7.4 0.1 fusion.11
  7.5 0.1 reduce_window_sum.11
  7.6 0.2 select_reduce_fusion
  7.8 0.7 add_select_fusion.2
  8.5 0.7 fusion.15
  9.2 0.1 broadcast_in_dim.19
  9.3 0.1 eq.83
  9.4 0.1 broadcast_in_dim.20
  9.5 1.3 convolution_convert_fusion
  10.8 1.0 reshape.112
  11.8 18.6 %all-to-all-start = ((bf16[64,4,1152]{2,1,0:T(4,128)(2,1)}), bf16[64,4,1152]{2,1,0:T(4,128)(2,1)S(1)}, u32[]{:S(2)}, u32[]{:S(2)}) async-start(bf16[64,4,1152]{2,1,0:T(4,128)(2,1)} %reshape.112), calls=%async_computation.1 | async-start | bytes 1179648 | tf_op jit(solution)/shard_map/all_to_all | solution.py:47
  30.5 0.1 select_n.32
  30.6 0.2 fusion
  30.7 120.6 %all-gather.1 = bf16[64,4,1152]{2,1,0:T(4,128)(2,1)S(1)} all-gather(bf16[1,4,1152]{2,1,0:T(4,128)(2,1)S(1)} %fusion), channel_id=1, replica_groups=mesh['ad'=64,'tp'=8] {'ad'}, dimensions={0}, use_global_device_ids=true | all-gather | bytes 599040 | tf_op jit(solution)/shard_map/all_gather | solution.py:46
  151.3 1.0 reshape.121
  152.3 2.5 %fusion.25 = f32[192,1024]{1,0:T(8,128)} fusion(bf16[192,1024]{1,0:T(8,128)(2,1)} %bitcast.29, bf16[1024,1024]{1,0:T(8,128)(2,1)S(1)} %copy-done), kind=kOutput, calls=%fused_computation.53 | convolution fusion | flops 402653184 | bytes 3276800 | tf_op jit(solution)/shard_map/dot_general | solution.py:48
  154.8 0.1 subtract_reduce_fusion
  155.0 1.0 reshape.113
  155.9 0.9 convert_reduce_fusion
  156.9 1.7 fusion.4
  158.6 0.7 multiply_reduce_fusion
  159.4 0.7 reduce-scatter.2.cloned.1.call-update
  160.1 29.5 %all-gather.4.cloned.1.call-done = f32[4096,64]{0,1:T(8,128)} async-done(((f32[512,64]{0,1:T(8,128)}), f32[4096,64]{0,1:T(8,128)}) %all-gather.4.cloned.1.call-update) | async-done | bytes 1048592 | tf_op jit(solution)/shard_map/all_gather | solution.py:66
  189.7 1.8 copy.6
  191.5 0.3 bitcast_reduce_fusion
  191.8 0.3 fusion.1
  192.2 32.5 %all_to_all.10 = bf16[64,8,128]{2,1,0:T(8,128)(2,1)S(1)} all-to-all(bf16[64,8,128]{2,1,0:T(8,128)(2,1)S(1)} %pad_maximum_fusion.5), channel_id=1, replica_groups=mesh['ad'=64,'tp'=8] {'ad'}, dimensions={0} | all-to-all | bytes 262144 | tf_op jit(solution)/shard_map/all_to_all | solution.py:79
  224.7 0.1 convert_reduce_fusion.1
  224.8 0.2 fusion.12
  225.0 7.4 %reduce-scatter.2.cloned.1.call-done = f32[192,128]{1,0:T(8,128)} async-done(((f32[192,1024]{1,0:T(8,128)}), f32[192,128]{1,0:T(8,128)}) %reduce-scatter.2.cloned.1.call-update) | async-done | bytes 98320 | tf_op jit(solution)/shard_map/reduce_scatter | solution.py:50
  232.4 1.8 fusion.3
  (18 shorter events, 0.3 us)
Async XLA Ops:
  6.5 145.8 %copy-start = (bf16[1024,1024]{1,0:T(8,128)(2,1)S(1)}, bf16[1024,1024]{1,0:T(8,128)(2,1)}, u32[]{:S(2)}) copy-start(bf16[1024,1024]{1,0:T(8,128)(2,1)} %param.7) | copy-start | bytes 6291460
  6.5 24.0 %copy-start.2 = (bf16[4,48,1024]{2,1,0:T(8,128)(2,1)S(1)}, bf16[4,48,1024]{2,1,0:T(8,128)(2,1)}, u32[]{:S(2)}) copy-start(bf16[4,48,1024]{2,1,0:T(8,128)(2,1)} %param.5) | copy-start | bytes 1179652
  11.8 143.2 %all-to-all-start = ((bf16[64,4,1152]{2,1,0:T(4,128)(2,1)}), bf16[64,4,1152]{2,1,0:T(4,128)(2,1)S(1)}, u32[]{:S(2)}, u32[]{:S(2)}) async-start(bf16[64,4,1152]{2,1,0:T(4,128)(2,1)} %reshape.112), calls=%async_computation.1 | async-start | bytes 1179648 | tf_op jit(solution)/shard_map/all_to_all | solution.py:47
  30.4 159.2 %all-gather.4.cloned.1.call-start = ((), (), s32[]{:S(2)}) async-start(), calls=%async_computation.4 | async-start | bytes 1179648 | tf_op jit(solution)/shard_map/all_gather | solution.py:66
  152.3 2.5 %copy-start.1 = (bf16[256,1152]{1,0:T(8,128)(2,1)S(1)}, bf16[256,1152]{1,0:T(8,128)(2,1)}, u32[]{:S(2)}) copy-start(bf16[256,1152]{1,0:T(8,128)(2,1)} %reshape.121) | copy-start | bytes 1769476
  159.3 32.4 %copy-start.3 = (bf16[4,64,128]{2,1,0:T(8,128)(2,1)S(1)}, bf16[4,64,128]{2,1,0:T(8,128)(2,1)}, u32[]{:S(2)}) copy-start(bf16[4,64,128]{2,1,0:T(8,128)(2,1)} %param.9) | copy-start | bytes 196612
  159.4 73.0 %reduce-scatter.2.cloned.1.call-start = ((), (), s32[]{:S(2)}) async-start(), calls=%async_computation.3 | async-start | bytes 884736 | tf_op jit(solution)/shard_map/reduce_scatter | solution.py:50
Sparse Core Ops, SparseCore 0:
  159.5 30.1 all-gather.3
  192.5 39.8 reduce-scatter.1
